TPU v7x, 32 devices: a whole 2x2x4 slice. The times are simulated.
32 devices in a mesh: head: 4 (over x, core), blk: 8 (over z, y).
Axes of the slice: x: 2, y: 2, z: 4, core: 2. Of those that a mesh axis runs over, the one named last changes fastest.
Arguments:
- inputs: bfloat16 [2, 2048, 768], P(None, ('blk', 'head')), may hold values from -6 to 6
- time_embed: float32 [2, 128], replicated, may hold values from -6 to 6
- segments: int32 [2, 2048], P(None, ('blk', 'head')), may hold values from 0 to 15, never falling along the last dimension, each value on 1 to 1280 neighbouring positions
- valid_mask: int32 [2, 2048], P(None, ('blk', 'head')), may hold values from 0 to 1
- teacher: bfloat16 [2, 2048, 768], P(None, ('blk', 'head')), may hold values from -6 to 6
- ada_weight: bfloat16 [128, 4608], P(None, ('head', 'blk')), may hold values from -0.25 to 0.25
- ada_bias: bfloat16 [4608], P(('head', 'blk')), may hold values from -3 to 3
- gain_attn: bfloat16 [768], P(('head', 'blk')), may hold values from 0.5 to 1.5
- qkv_weight: bfloat16 [768, 2304], P(('head', 'blk')), may hold values from -0.21875 to 0.21875
- out_weight: bfloat16 [768, 768], P(('head', 'blk')), may hold values from -3 to 3
- gain_mlp: bfloat16 [768], P(('head', 'blk')), may hold values from 0.5 to 1.5
- up_weight: bfloat16 [768, 3072], P(('head', 'blk')), may hold values from -0.21875 to 0.21875
- up_bias: bfloat16 [3072], P(('head', 'blk')), may hold values from -3 to 3
- down_weight: bfloat16 [3072, 768], P(('head', 'blk')), may hold values from -0.109375 to 0.109375
- down_bias: bfloat16 [768], P(('head', 'blk')), may hold values from -3 to 3
Outputs:
- output: bfloat16 [2, 2048, 768], P(None, ('blk', 'head'))
- loss_value: float32 [], replicated
- grad_input: float32 [2, 2048, 768], P(None, ('blk', 'head'))
- grad_ada_weight: float32 [128, 4608], P(None, ('head', 'blk'))
- grad_ada_bias: float32 [4608], P(('head', 'blk'))
- grad_gain_attn: float32 [768], P(('head', 'blk'))
- grad_qkv_weight: float32 [768, 2304], P(('head', 'blk'))
- grad_out_weight: float32 [768, 768], P(('head', 'blk'))
- grad_gain_mlp: float32 [768], P(('head', 'blk'))
- grad_up_weight: float32 [768, 3072], P(('head', 'blk'))
- grad_up_bias: float32 [3072], P(('head', 'blk'))
- grad_down_weight: float32 [3072, 768], P(('head', 'blk'))
- grad_down_bias: float32 [768], P(('head', 'blk'))
Inputs may be any that keep to these rules, and one draw needn't show every extreme that they name: `segments`: documents are numbered from 0 along each sequence, never falling; a document has 1 to 1280 tokens, and one has exactly that many.
All inputs are finite; a program needn't handle non-finite values.
Results may differ from a plain program's by a relative error of at most 0.019.
Values may be sent and summed in bfloat16 or wider, within the bound.
No kernel may reach another device: no remote copies, remote signals or barrier semaphores. Data moves between devices by JAX's collectives and lax.ppermute only.
A program may use at most 576 MiB of HBM per device.

v0:
```python
from functools import partial
import jax
import jax.numpy as jnp
from jax import lax
from jax.sharding import PartitionSpec as P

HEADS = 12
HEAD_DIM = 64
precise = lax.Precision.HIGHEST


def normalize(hidden):
    average = jnp.mean(hidden, axis=-1, keepdims=True)
    centred = hidden - average
    variance = jnp.mean(centred * centred, axis=-1, keepdims=True)
    inverse = lax.rsqrt(variance + 1e-05)
    return (centred * inverse, inverse)


def norm_back(upstream, normed, inverse):
    first_mean = jnp.mean(upstream, axis=-1, keepdims=True)
    second_mean = jnp.mean(upstream * normed, axis=-1, keepdims=True)
    return inverse * (upstream - first_mean - normed * second_mean)


def split_three(value):
    high_part = value.astype(jnp.bfloat16)
    rest = value - high_part.astype(jnp.float32)
    middle_part = rest.astype(jnp.bfloat16)
    last_part = (rest - middle_part.astype(jnp.float32)).astype(jnp.bfloat16)
    return jnp.stack([high_part, middle_part, last_part], axis=2)


def on_device(
    inputs,
    time_embed,
    segments,
    valid_mask,
    teacher,
    ada_weight,
    ada_bias,
    gain_attn,
    qkv_weight,
    out_weight,
    gain_mlp,
    up_weight,
    up_bias,
    down_weight,
    down_bias,
):
    seq_count, tokens, model_width = inputs.shape
    n_head = lax.axis_size("head")
    n_blk = lax.axis_size("blk")
    length = tokens * n_head * n_blk
    queries = tokens * n_head
    heads_here = HEADS // n_head
    local_width = heads_here * HEAD_DIM
    scale_factor = HEAD_DIM ** (-0.5)
    bf16 = jnp.bfloat16
    f32 = jnp.float32
    blk_here = lax.axis_index("blk")
    all_docs = lax.all_gather(segments, ("head", "blk"), axis=1, tiled=True)
    key_docs = (
        all_docs.reshape(seq_count, n_head, n_blk, tokens)
        .transpose(0, 2, 1, 3)
        .reshape(seq_count, length)
    )
    query_docs = lax.dynamic_slice_in_dim(key_docs, blk_here * queries, queries, 1)
    mask_float = valid_mask.astype(f32)
    count_here = jnp.sum(mask_float)
    gathered = (
        lax.all_gather(qkv_weight, ("head", "blk"), axis=0, tiled=True),
        lax.all_gather(out_weight, ("head", "blk"), axis=0, tiled=True),
        lax.all_gather(up_weight, ("head", "blk"), axis=0, tiled=True),
        lax.all_gather(down_weight, ("head", "blk"), axis=0, tiled=True),
        lax.all_gather(ada_weight, ("head", "blk"), axis=1, tiled=True),
        lax.all_gather(ada_bias, ("head", "blk"), axis=0, tiled=True),
        lax.all_gather(gain_attn, ("head", "blk"), axis=0, tiled=True),
        lax.all_gather(gain_mlp, ("head", "blk"), axis=0, tiled=True),
        lax.all_gather(up_bias, ("head", "blk"), axis=0, tiled=True),
        lax.all_gather(down_bias, ("head", "blk"), axis=0, tiled=True),
    )
    (
        full_qkv,
        full_out,
        full_up,
        full_down,
        full_ada,
        full_ada_bias,
        full_gain_attn,
        full_gain_mlp,
        full_up_bias,
        full_down_bias,
    ) = gathered
    gain_one = full_gain_attn.astype(f32)
    gain_two = full_gain_mlp.astype(f32)
    modulation = jnp.dot(
        time_embed, full_ada.astype(f32), precision=precise
    ) + full_ada_bias.astype(f32)
    pieces = modulation.reshape(seq_count, 6, 1, model_width)
    shift_attn = pieces[:, 0]
    scale_attn = pieces[:, 1]
    gate_attn = pieces[:, 2]
    shift_mlp = pieces[:, 3]
    scale_mlp = pieces[:, 4]
    gate_mlp = pieces[:, 5]
    residual = inputs.astype(f32)
    normed_one, inverse_one = normalize(residual)
    scaled_one = normed_one * gain_one
    entered = (scaled_one * (1.0 + scale_attn) + shift_attn).astype(bf16)
    triple = jnp.einsum("std,df->stf", entered, full_qkv, preferred_element_type=f32).astype(bf16)
    triple = triple.reshape(seq_count, tokens, 3, model_width)
    grouped = lax.all_to_all(triple, "head", split_axis=3, concat_axis=1, tiled=True)
    query_send = grouped[:, :, 0]
    query_heads = query_send.reshape(seq_count, queries, heads_here, HEAD_DIM).transpose(0, 2, 1, 3)
    key_rows = grouped[:, :, 1]
    value_rows = grouped[:, :, 2]

    def heads_first(part):
        part_rows = part.shape[1]
        return part.reshape(seq_count, part_rows, heads_here, HEAD_DIM).transpose(0, 2, 1, 3)

    def forward_step(running, arrived, first_row, live=True):
        row_max, denominator, numerator = running
        key_part, value_part = arrived
        part_rows = key_part.shape[1]
        key_four = heads_first(key_part)
        value_four = heads_first(value_part)
        allowed = jnp.logical_and(query_docs[:, :, None] == key_docs[:, None, :], live)[:, None]
        scores = (
            jnp.einsum("shqe,shke->shqk", query_heads, key_four, preferred_element_type=f32)
            * scale_factor
        )
        masked = jnp.where(allowed, scores, -1e30)
        new_max = jnp.maximum(row_max, jnp.max(masked, axis=-1))
        exponent = jnp.where(allowed, jnp.exp(scores - new_max[..., None]), 0.0)
        denominator = jnp.sum(exponent, axis=-1)
        numerator = jnp.einsum(
            "shqk,shke->shqe", exponent.astype(bf16), value_four, preferred_element_type=f32
        )
        return (new_max, denominator, numerator)

    start_state = (
        jnp.full((seq_count, heads_here, queries), -1e30, f32),
        jnp.zeros((seq_count, heads_here, queries), f32),
        jnp.zeros((seq_count, heads_here, queries, HEAD_DIM), f32),
    )
    row_max, denominator, numerator = forward_step(
        start_state,
        (
            lax.all_gather(key_rows, "blk", axis=1, tiled=True),
            lax.all_gather(value_rows, "blk", axis=1, tiled=True),
        ),
        jnp.int32(0),
    )
    attention = numerator / denominator[..., None]
    log_total = row_max + jnp.log(denominator)
    attn_send = (
        attention.astype(bf16).transpose(0, 2, 1, 3).reshape(seq_count, queries, local_width)
    )
    mixed = lax.all_to_all(attn_send, "head", split_axis=1, concat_axis=2, tiled=True)
    branch = jnp.einsum("std,de->ste", mixed, full_out, preferred_element_type=f32)
    hidden = residual + gate_attn * branch
    normed_two, inverse_two = normalize(hidden)
    scaled_two = normed_two * gain_two
    moved = (scaled_two * (1.0 + scale_mlp) + shift_mlp).astype(bf16)
    upper_in = jnp.einsum(
        "std,df->stf", moved, full_up, preferred_element_type=f32
    ) + full_up_bias.astype(f32)
    active = jax.nn.gelu(upper_in, approximate=True).astype(bf16)
    lower_out = jnp.einsum(
        "stf,fd->std", active, full_down, preferred_element_type=f32
    ) + full_down_bias.astype(f32)
    final_state = hidden + gate_mlp * lower_out
    mismatch = final_state - teacher.astype(f32)
    error_here = jnp.sum(mask_float[:, :, None] * mismatch * mismatch)
    error_all, count_all = lax.psum((error_here, count_here), ("head", "blk"))
    loss_value = error_all / (count_all * model_width)
    grad_final = seq_count * length / count_all * mask_float[:, :, None] * mismatch
    grad_lower = (gate_mlp * grad_final).astype(bf16)
    grad_gate_mlp = jnp.sum(grad_final * lower_out, axis=1)
    grad_down_weight = jnp.einsum("stf,std->fd", active, grad_lower, preferred_element_type=f32)
    grad_down_bias = jnp.sum(grad_lower.astype(f32), axis=(0, 1))
    grad_active = jnp.einsum("std,fd->stf", grad_lower, full_down, preferred_element_type=f32)
    unused_value, gelu_back = jax.vjp(partial(jax.nn.gelu, approximate=True), upper_in)
    grad_upper = gelu_back(grad_active)[0].astype(bf16)
    grad_up_weight = jnp.einsum("std,stf->df", moved, grad_upper, preferred_element_type=f32)
    grad_up_bias = jnp.sum(grad_upper.astype(f32), axis=(0, 1))
    grad_moved = jnp.einsum("stf,df->std", grad_upper, full_up, preferred_element_type=f32)
    grad_shift_mlp = jnp.sum(grad_moved, axis=1)
    grad_scale_mlp = jnp.sum(grad_moved * scaled_two, axis=1)
    grad_scaled_two = grad_moved * (1.0 + scale_mlp)
    grad_gain_mlp = jnp.sum(grad_scaled_two * normed_two, axis=(0, 1))
    grad_hidden = grad_final + norm_back(grad_scaled_two * gain_two, normed_two, inverse_two)
    grad_branch = (gate_attn * grad_hidden).astype(bf16)
    grad_gate_attn = jnp.sum(grad_hidden * branch, axis=1)
    grad_out_weight = jnp.einsum("ste,std->ed", mixed, grad_branch, preferred_element_type=f32)
    grad_mixed = jnp.einsum(
        "std,ed->ste", grad_branch, full_out, preferred_element_type=f32
    ).astype(bf16)
    grad_heads = lax.all_to_all(grad_mixed, "head", split_axis=2, concat_axis=1, tiled=True)
    grad_four = heads_first(grad_heads)
    row_delta = jnp.sum(grad_four.astype(f32) * attention, axis=-1)

    def query_step(running, arrived, first_row, live=True):
        key_part, value_part = arrived
        part_rows = key_part.shape[1]
        key_four = heads_first(key_part)
        value_four = heads_first(value_part)
        allowed = jnp.logical_and(query_docs[:, :, None] == key_docs[:, None, :], live)[:, None]
        scores = (
            jnp.einsum("shqe,shke->shqk", query_heads, key_four, preferred_element_type=f32)
            * scale_factor
        )
        probabilities = jnp.where(allowed, jnp.exp(scores - log_total[..., None]), 0.0)
        grad_probs = jnp.einsum(
            "shqe,shke->shqk", grad_four, value_four, preferred_element_type=f32
        )
        grad_scores = (probabilities * (grad_probs - row_delta[..., None])).astype(bf16)
        return (
            jnp.einsum("shqk,shke->shqe", grad_scores, key_four, preferred_element_type=f32)
            * scale_factor
        )

    key_local = heads_first(key_rows)
    value_local = heads_first(value_rows)

    def key_step(running, arrived, first_row, live=True):
        query_part, grad_part, stat_part = arrived
        part_rows = query_part.shape[1]
        query_low = heads_first(query_part)
        grad_low = heads_first(grad_part)
        stats = jnp.sum(
            stat_part.astype(f32).reshape(seq_count, part_rows, 2, 3, heads_here), axis=3
        )
        total_part = stats[:, :, 0].transpose(0, 2, 1)
        delta_part = stats[:, :, 1].transpose(0, 2, 1)
        allowed = jnp.logical_and(key_docs[:, :, None] == query_docs[:, None, :], live)[:, None]
        scores = (
            jnp.einsum("shqe,shke->shqk", query_low, key_local, preferred_element_type=f32)
            * scale_factor
        )
        probabilities = jnp.where(allowed, jnp.exp(scores - total_part[..., None]), 0.0)
        grad_probs = jnp.einsum(
            "shqe,shke->shqk", grad_low, value_local, preferred_element_type=f32
        )
        grad_scores = (probabilities * (grad_probs - delta_part[..., None])).astype(bf16)
        grad_value = jnp.einsum(
            "shqk,shqe->shke", probabilities.astype(bf16), grad_low, preferred_element_type=f32
        )
        grad_key = (
            jnp.einsum("shqk,shqe->shke", grad_scores, query_low, preferred_element_type=f32)
            * scale_factor
        )
        return (grad_key, grad_value)

    total_rows = log_total.transpose(0, 2, 1)
    delta_rows = row_delta.transpose(0, 2, 1)
    stat_send = jnp.stack([split_three(total_rows), split_three(delta_rows)], axis=2).reshape(
        seq_count, queries, 6 * heads_here
    )
    empty_grad = jnp.zeros((seq_count, heads_here, queries, HEAD_DIM), f32)
    grad_query = query_step(
        empty_grad,
        (
            lax.all_gather(key_rows, "blk", axis=1, tiled=True),
            lax.all_gather(value_rows, "blk", axis=1, tiled=True),
        ),
        jnp.int32(0),
    )
    grad_key, grad_value = key_step(
        (empty_grad, empty_grad),
        (
            lax.all_gather(query_send, "blk", axis=1, tiled=True),
            lax.all_gather(grad_heads, "blk", axis=1, tiled=True),
            lax.all_gather(stat_send, "blk", axis=1, tiled=True),
        ),
        jnp.int32(0),
    )

    def rows_first(value):
        return value.transpose(0, 2, 1, 3).reshape(seq_count, queries, local_width)

    grad_triple = jnp.stack(
        [rows_first(grad_query), rows_first(grad_key), rows_first(grad_value)], axis=2
    ).astype(bf16)
    grad_tokens = lax.all_to_all(grad_triple, "head", split_axis=1, concat_axis=3, tiled=True)
    grad_flat = grad_tokens.reshape(seq_count, tokens, 3 * model_width)
    grad_qkv_weight = jnp.einsum("std,stf->df", entered, grad_flat, preferred_element_type=f32)
    grad_entered = jnp.einsum("stf,df->std", grad_flat, full_qkv, preferred_element_type=f32)
    grad_shift_attn = jnp.sum(grad_entered, axis=1)
    grad_scale_attn = jnp.sum(grad_entered * scaled_one, axis=1)
    grad_scaled_one = grad_entered * (1.0 + scale_attn)
    grad_gain_attn = jnp.sum(grad_scaled_one * normed_one, axis=(0, 1))
    grad_input = grad_hidden + norm_back(grad_scaled_one * gain_one, normed_one, inverse_one)
    grad_modulation = jnp.stack(
        [
            grad_shift_attn,
            grad_scale_attn,
            grad_gate_attn,
            grad_shift_mlp,
            grad_scale_mlp,
            grad_gate_mlp,
        ],
        axis=1,
    ).reshape(seq_count, 6 * model_width)
    grad_ada_weight = jnp.dot(time_embed.T, grad_modulation, precision=precise)
    grad_ada_bias = jnp.sum(grad_modulation, axis=0)
    later_owned = (
        lax.psum_scatter(grad_out_weight, ("head", "blk"), scatter_dimension=0, tiled=True),
        lax.psum_scatter(grad_up_weight, ("head", "blk"), scatter_dimension=0, tiled=True),
        lax.psum_scatter(grad_down_weight, ("head", "blk"), scatter_dimension=0, tiled=True),
        lax.psum_scatter(grad_gain_mlp, ("head", "blk"), scatter_dimension=0, tiled=True),
        lax.psum_scatter(grad_up_bias, ("head", "blk"), scatter_dimension=0, tiled=True),
        lax.psum_scatter(grad_down_bias, ("head", "blk"), scatter_dimension=0, tiled=True),
    )
    shard_out, shard_up, shard_down, shard_gain_mlp, shard_up_bias, shard_down_bias = later_owned
    first_owned = (
        lax.psum_scatter(grad_qkv_weight, ("head", "blk"), scatter_dimension=0, tiled=True),
        lax.psum_scatter(grad_ada_weight, ("head", "blk"), scatter_dimension=1, tiled=True),
        lax.psum_scatter(grad_ada_bias, ("head", "blk"), scatter_dimension=0, tiled=True),
        lax.psum_scatter(grad_gain_attn, ("head", "blk"), scatter_dimension=0, tiled=True),
    )
    shard_qkv, shard_ada, shard_ada_bias, shard_gain_attn = first_owned
    return (
        final_state.astype(bf16),
        loss_value,
        grad_input,
        shard_ada,
        shard_ada_bias,
        shard_gain_attn,
        shard_qkv,
        shard_out,
        shard_gain_mlp,
        shard_up,
        shard_up_bias,
        shard_down,
        shard_down_bias,
    )


def solution(mesh):
    return jax.shard_map(
        on_device,
        mesh=mesh,
        in_specs=(
            P(None, ("blk", "head"), None),
            P(),
            P(None, ("blk", "head")),
            P(None, ("blk", "head")),
            P(None, ("blk", "head"), None),
            P(None, ("head", "blk")),
            P(("head", "blk")),
            P(("head", "blk")),
            P(("head", "blk"), None),
            P(("head", "blk"), None),
            P(("head", "blk")),
            P(("head", "blk"), None),
            P(("head", "blk")),
            P(("head", "blk"), None),
            P(("head", "blk")),
        ),
        out_specs=(
            P(None, ("blk", "head"), None),
            P(),
            P(None, ("blk", "head"), None),
            P(None, ("head", "blk")),
            P(("head", "blk")),
            P(("head", "blk")),
            P(("head", "blk"), None),
            P(("head", "blk"), None),
            P(("head", "blk")),
            P(("head", "blk"), None),
            P(("head", "blk")),
            P(("head", "blk"), None),
            P(("head", "blk")),
        ),
        check_vma=False,
    )
```

profile of v0, /device:TPU:0, one launch (start us, length us, event | category | flops | bytes accessed | tf_op | source)
XLA Modules:
  0.0 1162.7 jit_solution(6677036301440943555)
XLA Ops:
  13.0 42.4 %all-reduce.11 = (bf16[4608]{0:T(1024)(128)(2,1)S(1)}, bf16[768]{0:T(1024)(128)(2,1)S(1)}, bf16[768]{0:T(1024)(128)(2,1)S(1)}, bf16[3072]{0:T(1024)(128)(2,1)S(1)}, bf16[768]{0:T(1024)(128)(2,1)S(1)}) all-reduce(bf16[4608]{0:T(1024)(128)(2,1)S(1)} %dynamic-update-slice, ...), channel_id=1, replica_groups=mesh['head'=4,'blk'=8] {'head','blk'}, use_global_device_ids=true, to_apply=%add | all-reduce | flops 9984 | bytes 39936
  57.6 10.2 all-gather.14.cloned.1.call-done
  70.2 59.7 %all-gather.16.cloned.1.call-done = bf16[768,2304]{1,0:T(8,128)(2,1)} async-done(((bf16[24,2304]{1,0:T(8,128)(2,1)}), bf16[768,2304]{1,0:T(8,128)(2,1)}) %all-gather.16.cloned.1.call-update) | async-done | bytes 3538960 | tf_op jit(solution)/shard_map/all_gather | solution.py:72
  135.3 12.0 %all_to_all.69 = bf16[4,2,36864]{2,1,0:T(2,128)(2,1)S(1)} all-to-all(bf16[4,2,36864]{2,1,0:T(2,128)(2,1)S(1)} %reshape.208), channel_id=1, replica_groups=mesh['head'=4,'blk'=8] {'head'}, dimensions={0} | all-to-all | bytes 1179648 | tf_op jit(solution)/shard_map/all_to_all | solution.py:113
  154.6 39.7 %psum.15 = f32[]{:T(128)} all-reduce(f32[]{:T(128)} %convert_reduce_fusion.4), channel_id=1, replica_groups=mesh['head'=4,'blk'=8] {'head','blk'}, use_global_device_ids=true, to_apply=%region_9.10 | all-reduce | flops 1 | bytes 8 | tf_op jit(solution)/shard_map/psum | solution.py:177
  194.3 66.7 %all-gather.3 = s32[32,64,2]{1,2,0:T(2,128)S(1)} all-gather(s32[1,64,2]{1,2,0:T(2,128)S(1)} %bitcast.271), channel_id=1, replica_groups=mesh['head'=4,'blk'=8] {'head','blk'}, dimensions={0}, use_global_device_ids=true | all-gather | bytes 16896 | tf_op jit(solution)/shard_map/all_gather | solution.py:62
  265.8 4.4 copy.137
  270.2 5.9 select_reduce_fusion
  276.1 7.0 fusion
  283.1 7.0 fusion.75
  295.3 5.0 all-to-all-done.1
  300.8 5.0 all-gather.18.cloned.1.call-done
  308.4 62.9 %all-gather.20.cloned.1.call-done = bf16[768,3072]{1,0:T(8,128)(2,1)} async-done(((bf16[24,3072]{1,0:T(8,128)(2,1)}), bf16[768,3072]{1,0:T(8,128)(2,1)}) %all-gather.20.cloned.1.call-update) | async-done | bytes 4718608 | tf_op jit(solution)/shard_map/all_gather | solution.py:74
  374.6 62.2 %all-gather.22.cloned.1.call-done = bf16[3072,768]{1,0:T(8,128)(2,1)} async-done(((bf16[96,768]{1,0:T(8,128)(2,1)}), bf16[3072,768]{1,0:T(8,128)(2,1)}) %all-gather.22.cloned.1.call-update) | async-done | bytes 4718608 | tf_op jit(solution)/shard_map/all_gather | solution.py:75
  436.8 4.9 convert_reduce_fusion.2
  452.3 9.4 all_to_all.70
  470.2 17.1 %all-gather.30.cloned.1.call-done = bf16[2,2048,1,192]{3,1,2,0:T(8,128)(2,1)} async-done(((bf16[2,256,1,192]{3,1,2,0:T(8,128)(2,1)}), bf16[2,2048,1,192]{3,1,2,0:T(8,128)(2,1)}) %all-gather.30.cloned.1.call-update) | async-done | bytes 1572880 | tf_op jit(solution)/shard_map/all_gather | solution.py:274
  491.3 7.8 fusion.101
  504.7 12.0 %fusion.52 = bf16[2,3,256,64]{2,3,1,0:T(8,128)(2,1)} fusion(bf16[2,3,2048,64]{2,3,1,0:T(8,128)(2,1)} %bitcast.231, f32[2,3,256,2048]{3,2,1,0:T(8,128)} %get-tuple-element.63, f32[2,3,256]{2,1,0:T(4,128)S(1)} %multiply_reduce_fusion.4, f32[2,3,256]{2,1,0:T(4,128)S(1)} %log_add_fusion, pred[2,256,2048]{2,1,0:T(8,128)(4,1)S(1)} %broadcast_compare_fusion.1, ...), kind=kOutput, calls=%fused_computation.58 | convolution fusion | flops 824377344 | bytes 17182720 | tf_op jit(solution)/shard_map/shqk,shke->shqe/dot_general | solution.py:221
  517.9 20.8 %all_gather.64 = bf16[2,2048,18]{1,0,2:T(2,128)(2,1)S(1)} all-gather(bf16[2,256,18]{1,0,2:T(2,128)(2,1)S(1)} %bitcast.268), channel_id=1, replica_groups=mesh['head'=4,'blk'=8] {'blk'}, dimensions={1}, use_global_device_ids=true | all-gather | bytes 165888 | tf_op jit(solution)/shard_map/all_gather | solution.py:276
  544.2 11.6 fusion.53
  557.6 7.4 fusion.54
  568.3 14.2 %all_to_all.71 = bf16[2,256,3,192]{3,0,2,1:T(2,128)(2,1)S(1)} all-to-all(bf16[2,256,3,192]{3,0,2,1:T(2,128)(2,1)S(1)} %pad_maximum_fusion), channel_id=1, replica_groups=mesh['head'=4,'blk'=8] {'head'}, dimensions={1} | all-to-all | bytes 1179648 | tf_op jit(solution)/shard_map/all_to_all | solution.py:287
  584.0 4.7 fusion.72
  589.4 5.2 convolution_bitcast_fusion
  594.8 5.9 convolution_bitcast_fusion.2
  601.6 5.2 convolution_bitcast_fusion.1
  612.6 39.1 %all-reduce.10 = (f32[]{:T(128)}, f32[4608]{0:T(1024)S(1)}, f32[768]{0:T(1024)S(1)}, f32[768]{0:T(1024)S(1)}, f32[3072]{0:T(1024)S(1)}, /*index=5*/f32[768]{0:T(1024)S(1)}) all-reduce(f32[]{:T(128)} %get-tuple-element.47, f32[4608]{0:T(1024)S(1)} %reduce_sum.238, ...), channel_id=1, replica_groups=mesh['head'=4,'blk'=8] {'head','blk'}, use_global_device_ids=true, to_apply=%region_7.8 | all-reduce | flops 9985 | bytes 79880 | tf_op jit(solution)/shard_map/psum | solution.py:177
  656.4 91.1 %reduce-scatter.6.cloned.1.call-done = f32[128,144]{0,1:T(8,128)} async-done(((f32[128,4608]{0,1:T(8,128)}), f32[128,144]{0,1:T(8,128)}) %reduce-scatter.6.cloned.1.call-update) | async-done | bytes 73744 | tf_op jit(solution)/shard_map/reduce_scatter | solution.py:320
  747.4 140.9 %reduce-scatter.12.cloned.1.call-done = f32[24,3072]{1,0:T(8,128)} async-done(((f32[768,3072]{1,0:T(8,128)}), f32[24,3072]{1,0:T(8,128)}) %reduce-scatter.12.cloned.1.call-update) | async-done | bytes 294928 | tf_op jit(solution)/shard_map/reduce_scatter | solution.py:311
  888.3 142.2 %reduce-scatter.14.cloned.1.call-done = f32[96,768]{1,0:T(8,128)} async-done(((f32[3072,768]{1,0:T(8,128)}), f32[96,768]{1,0:T(8,128)}) %reduce-scatter.14.cloned.1.call-update) | async-done | bytes 294928 | tf_op jit(solution)/shard_map/reduce_scatter | solution.py:312
  1030.5 124.3 %reduce-scatter.8.cloned.1.call-done = f32[24,2304]{1,0:T(8,128)} async-done(((f32[768,2304]{1,0:T(8,128)}), f32[24,2304]{1,0:T(8,128)}) %reduce-scatter.8.cloned.1.call-update) | async-done | bytes 221200 | tf_op jit(solution)/shard_map/reduce_scatter | solution.py:319
  (250 shorter events, 90.4 us)
Async XLA Ops:
  7.2 60.6 %copy-start = (f32[2,128]{1,0:T(2,128)S(1)}, f32[2,128]{1,0:T(2,128)}, u32[]{:S(2)}) copy-start(f32[2,128]{1,0:T(2,128)} %param.16) | copy-start | bytes 3076
  7.2 122.7 %copy-start.1 = (bf16[2,64,768]{2,1,0:T(8,128)(2,1)S(1)}, bf16[2,64,768]{2,1,0:T(8,128)(2,1)}, u32[]{:S(2)}) copy-start(bf16[2,64,768]{2,1,0:T(8,128)(2,1)} %param.15) | copy-start | bytes 589828
  7.2 60.6 %all-gather.14.cloned.1.call-start = ((), (), s32[]{:S(2)}) async-start(), calls=%async_computation.9 | async-start | bytes 1216512 | tf_op jit(solution)/shard_map/all_gather | solution.py:76
  7.9 122.0 %all-gather.16.cloned.1.call-start = ((), (), s32[]{:S(2)}) async-start(), calls=%async_computation.10 | async-start | bytes 3649536 | tf_op jit(solution)/shard_map/all_gather | solution.py:72
  8.7 254.2 %all-gather.26.cloned.1.call-start = ((), (), s32[]{:S(2)}) async-start(), calls=%async_computation.20 | async-start | bytes 2359296 | tf_op jit(solution)/shard_map/all_gather | solution.py:151
  56.4 76.2 %copy-start.31 = (f32[2,64]{1,0:T(2,128)}, f32[2,64]{1,0:T(2,128)S(1)}, u32[]{:S(2)}) copy-start(f32[2,64]{1,0:T(2,128)S(1)} %broadcast_multiply_fusion.6) | copy-start | bytes 1540
  57.6 75.1 %copy-start.33 = (f32[2,64]{1,0:T(2,128)}, f32[2,64]{1,0:T(2,128)S(1)}, u32[]{:S(2)}) copy-start(f32[2,64]{1,0:T(2,128)S(1)} %add_rsqrt_fusion.1) | copy-start | bytes 1540
  70.2 62.4 %copy-start.24 = (f32[2,1,1,768]{3,0,1,2:T(2,128)}, f32[2,1,1,768]{3,0,1,2:T(2,128)S(1)}, u32[]{:S(2)}) copy-start(f32[2,1,1,768]{3,0,1,2:T(2,128)S(1)} %copy.171) | copy-start | bytes 18436
  70.2 62.4 %copy-start.26 = (f32[2,1,1,768]{3,0,1,2:T(2,128)}, f32[2,1,1,768]{3,0,1,2:T(2,128)S(1)}, u32[]{:S(2)}) copy-start(f32[2,1,1,768]{3,0,1,2:T(2,128)S(1)} %copy.170) | copy-start | bytes 18436
  150.4 43.8 %copy-start.46 = (s32[2,64]{1,0:T(2,128)S(1)}, s32[2,64]{1,0:T(2,128)}, u32[]{:S(2)}) copy-start(s32[2,64]{1,0:T(2,128)} %param.17) | copy-start | bytes 1540
  151.4 114.3 %copy-start.11 = (bf16[2,256,1,192]{3,1,2,0:T(8,128)(2,1)}, bf16[2,256,1,192]{3,1,2,0:T(8,128)(2,1)S(1)}, u32[]{:S(2)}) copy-start(bf16[2,256,1,192]{3,1,2,0:T(8,128)(2,1)S(1)} %get-tuple-element.46) | copy-start | bytes 589828
  151.5 114.3 %all-gather.28.cloned.1.call-start = ((), (), s32[]{:S(2)}) async-start(), calls=%async_computation.21 | async-start | bytes 2359296 | tf_op jit(solution)/shard_map/all_gather | solution.py:152
  152.0 153.8 %all-gather.18.cloned.1.call-start = ((), (), s32[]{:S(2)}) async-start(), calls=%async_computation.11 | async-start | bytes 1216512 | tf_op jit(solution)/shard_map/all_gather | solution.py:73
  152.6 218.7 %all-gather.20.cloned.1.call-start = ((), (), s32[]{:S(2)}) async-start(), calls=%async_computation.12 | async-start | bytes 4866048 | tf_op jit(solution)/shard_map/all_gather | solution.py:74
  153.2 283.6 %all-gather.22.cloned.1.call-start = ((), (), s32[]{:S(2)}) async-start(), calls=%async_computation.13 | async-start | bytes 4866048 | tf_op jit(solution)/shard_map/all_gather | solution.py:75
  290.9 9.4 all-to-all-start.1
  294.3 193.0 %all-gather.30.cloned.1.call-start = ((), (), s32[]{:S(2)}) async-start(), calls=%async_computation.22 | async-start | bytes 2359296 | tf_op jit(solution)/shard_map/all_gather | solution.py:274
  294.4 77.0 %copy-start.28 = (f32[2,768]{1,0:T(2,128)}, f32[2,768]{1,0:T(2,128)S(1)}, u32[]{:S(2)}) copy-start(f32[2,768]{1,0:T(2,128)S(1)} %get-tuple-element.72) | copy-start | bytes 18436
  294.4 152.3 %copy-start.19 = (f32[2,768]{1,0:T(2,128)}, f32[2,768]{1,0:T(2,128)S(1)}, u32[]{:S(2)}) copy-start(f32[2,768]{1,0:T(2,128)S(1)} %get-tuple-element.73) | copy-start | bytes 18436
  295.1 245.2 %all-gather.24.cloned.1.call-start = ((), (), s32[]{:S(2)}) async-start(), calls=%async_computation.14 | async-start | bytes 2359296 | tf_op jit(solution)/shard_map/all_gather | solution.py:275
  300.8 70.5 %copy-start.12 = (bf16[2,64,768]{2,1,0:T(8,128)(2,1)}, bf16[2,64,768]{2,1,0:T(8,128)(2,1)S(1)}, u32[]{:S(2)}) copy-start(bf16[2,64,768]{2,1,0:T(8,128)(2,1)S(1)} %all_to_all.57) | copy-start | bytes 589828
  308.4 138.4 %copy-start.29 = (f32[2,64]{1,0:T(2,128)}, f32[2,64]{1,0:T(2,128)S(1)}, u32[]{:S(2)}) copy-start(f32[2,64]{1,0:T(2,128)S(1)} %add_rsqrt_fusion) | copy-start | bytes 1540
  465.5 190.9 %reduce-scatter.10.cloned.1.call-start = ((), (), s32[]{:S(2)}) async-start(), calls=%async_computation.17 | async-start | bytes 2433024 | tf_op jit(solution)/shard_map/reduce_scatter | solution.py:310
  470.2 21.0 %copy-start.17 = (bf16[2,256,1,192]{1,3,0,2:T(8,128)(2,1)S(1)}, bf16[2,256,1,192]{1,3,0,2:T(8,128)(2,1)}, u32[]{:S(2)}) copy-start(bf16[2,256,1,192]{1,3,0,2:T(8,128)(2,1)} %copy.145) | copy-start | bytes 589828
  501.0 246.4 %reduce-scatter.6.cloned.1.call-start = ((), (), s32[]{:S(2)}) async-start(), calls=%async_computation.15 | async-start | bytes 2433024 | tf_op jit(solution)/shard_map/reduce_scatter | solution.py:320
  594.7 293.6 %reduce-scatter.12.cloned.1.call-start = ((), (), s32[]{:S(2)}) async-start(), calls=%async_computation.18 | async-start | bytes 9732096 | tf_op jit(solution)/shard_map/reduce_scatter | solution.py:311
  600.7 429.8 %reduce-scatter.14.cloned.1.call-start = ((), (), s32[]{:S(2)}) async-start(), calls=%async_computation.19 | async-start | bytes 9732096 | tf_op jit(solution)/shard_map/reduce_scatter | solution.py:312
  606.8 548.0 %reduce-scatter.8.cloned.1.call-start = ((), (), s32[]{:S(2)}) async-start(), calls=%async_computation.16 | async-start | bytes 7299072 | tf_op jit(solution)/shard_map/reduce_scatter | solution.py:319
  611.7 43.7 %copy-start.48 = (f32[2,64]{1,0:T(2,128)S(1)}, f32[2,64]{1,0:T(2,128)}, u32[]{:S(2)}) copy-start(f32[2,64]{1,0:T(2,128)} %get-tuple-element.17) | copy-start | bytes 1540
  611.7 43.7 %copy-start.47 = (f32[2,64]{1,0:T(2,128)S(1)}, f32[2,64]{1,0:T(2,128)}, u32[]{:S(2)}) copy-start(f32[2,64]{1,0:T(2,128)} %get-tuple-element.19) | copy-start | bytes 1540
  611.7 43.7 %copy-start.5 = (f32[2,64,768]{2,1,0:T(8,128)S(1)}, f32[2,64,768]{2,1,0:T(8,128)}, u32[]{:S(2)}) copy-start(f32[2,64,768]{2,1,0:T(8,128)} %copy-done.3) | copy-start | bytes 1179652
  611.7 43.7 %copy-start.18 = (f32[2,64,768]{2,1,0:T(8,128)S(1)}, f32[2,64,768]{2,1,0:T(8,128)}, u32[]{:S(2)}) copy-start(f32[2,64,768]{2,1,0:T(8,128)} %get-tuple-element.69) | copy-start | bytes 1179652
  (35 other events, 146.3 us)
Sparse Core Ops, SparseCore 0:
  11.0 56.8 all-gather.13
  70.7 59.1 all-gather.15
  151.6 47.5 all-gather.25
  201.8 48.6 all-gather.27
  253.3 52.5 all-gather.17
  308.6 62.6 all-gather.19
  374.3 62.4 all-gather.21
  439.0 48.3 all-gather.29
  489.5 49.7 all-gather.23
  545.0 97.6 reduce-scatter.9
  649.4 97.9 reduce-scatter.5
  753.8 134.5 reduce-scatter.11
  895.8 134.6 reduce-scatter.13
  1036.6 118.1 reduce-scatter.7
where the time goes:
time: 1170 us; the launch traced here: 1160 us
  waiting for transfers between devices  725 us (62%)
  blocking collectives  244 us (21%)
  matrix products  99.8 us (9%)
  local copies, waits for them, and re-layouts  52.4 us (4%)
  other arithmetic  18.4 us (2%)
  between operations  18.2 us (2%)
    reduce_scatter x1, waiting for transfers between devices, on_device(): lax.psum_scatter(grad_down_weight, ('head', 'blk'), scatter_dimension=0,...  142 us
    reduce_scatter x1, waiting for transfers between devices, on_device(): lax.psum_scatter(grad_up_weight, ('head', 'blk'), scatter_dimension=0, ti...  141 us
    reduce_scatter x1, waiting for transfers between devices, on_device(): lax.psum_scatter(grad_qkv_weight, ('head', 'blk'), scatter_dimension=0, t...  124 us
    reduce_scatter x1, waiting for transfers between devices, on_device(): lax.psum_scatter(grad_ada_weight, ('head', 'blk'), scatter_dimension=1, t...  91.1 us
    psum x2, blocking collectives, on_device(): error_all, count_all = lax.psum((error_here, count_here), ('head', 'blk'))  78.8 us
    all_gather x1, blocking collectives, on_device(): all_docs = lax.all_gather(segments, ('head', 'blk'), axis=1, tiled=True)  66.7 us
    all_gather x1, waiting for transfers between devices, on_device(): lax.all_gather(up_weight, ('head', 'blk'), axis=0, tiled=True)  62.9 us
    all_gather x1, waiting for transfers between devices, on_device(): lax.all_gather(down_weight, ('head', 'blk'), axis=0, tiled=True)  62.2 us
  transfers between devices with their start and end apart: 15, of which 11 were waited for; matrix products, arithmetic and copies ran while one was open for 14% of the time, Pallas kernels for 0%

commit v1 on v0

--- a/solution.py
+++ b/solution.py
@@ -7,6 +7,28 @@
 HEADS = 12
 HEAD_DIM = 64
 precise = lax.Precision.HIGHEST
+
+
+def meet_scenes(local_x, k_dim):
+    chip_axis = ("head", "blk")
+    parts_out, w_next, x_next = (
+        lax.axis_size(chip_axis),
+        lax.axis_index(chip_axis),
+        local_x.shape[k_dim],
+    )
+    a_now, f_now = (local_x, 1)
+    while f_now < parts_out:
+        a_now = jnp.concatenate(
+            [
+                a_now,
+                lax.ppermute(
+                    a_now, chip_axis, [(dd, (dd - f_now) % parts_out) for dd in range(parts_out)]
+                ),
+            ],
+            axis=k_dim,
+        )
+        f_now = 2 * f_now
+    return jnp.roll(a_now, w_next * x_next, axis=k_dim)
 
 
 def normalize(hidden):
@@ -69,7 +91,7 @@
     mask_float = valid_mask.astype(f32)
     count_here = jnp.sum(mask_float)
     gathered = (
-        lax.all_gather(qkv_weight, ("head", "blk"), axis=0, tiled=True),
+        meet_scenes(qkv_weight, 0),
         lax.all_gather(out_weight, ("head", "blk"), axis=0, tiled=True),
         lax.all_gather(up_weight, ("head", "blk"), axis=0, tiled=True),
         lax.all_gather(down_weight, ("head", "blk"), axis=0, tiled=True),

time: 1170 us -> 1190 us (1.017)
  waiting for transfers between devices: 725 us -> 688 us
  blocking collectives: 244 us -> 277 us
  local copies, waits for them, and re-layouts: 52.4 us -> 69.6 us
    all_gather x1 -> x0, waiting for transfers between devices: 59.7 us -> none  [on_device(): lax.all_gather(qkv_weight, ('head', 'blk'), axis=0, tiled=True)]
    ppermute x0 -> x5, waiting for transfers between devices: none -> 39 us  [meet_scenes(): lax.ppermute(a_now, chip_axis, [(dd, (dd - f_now) % parts_out) for dd in...]
    unnamed x1, blocking collectives: 42.4 us -> 77.1 us
  transfers between devices with their start and end apart: 15 -> 19, of which waited for: 11 -> 13; matrix products, arithmetic and copies ran while one was open for 14% -> 14% of each run, Pallas kernels for 0% -> 0%
where the time goes in v1:
time: 1190 us
  waiting for transfers between devices  688 us (58%)
  blocking collectives  277 us (23%)
  matrix products  99.7 us (8%)
  local copies, waits for them, and re-layouts  69.6 us (6%)
  other arithmetic  20.6 us (2%)
  between operations  18 us (2%)
  starting transfers between devices  13.3 us (1%)
    reduce_scatter x1, waiting for transfers between devices, on_device(): lax.psum_scatter(grad_down_weight, ('head', 'blk'), scatter_dimension=0,...  142 us
    reduce_scatter x1, waiting for transfers between devices, on_device(): lax.psum_scatter(grad_up_weight, ('head', 'blk'), scatter_dimension=0, ti...  141 us
    reduce_scatter x1, waiting for transfers between devices, on_device(): lax.psum_scatter(grad_qkv_weight, ('head', 'blk'), scatter_dimension=0, t...  124 us
    reduce_scatter x1, waiting for transfers between devices, on_device(): lax.psum_scatter(grad_ada_weight, ('head', 'blk'), scatter_dimension=1, t...  86.9 us
    unnamed x1, blocking collectives  77.1 us
    psum x2, blocking collectives, on_device(): error_all, count_all = lax.psum((error_here, count_here), ('head', 'blk'))  76.7 us
    all_gather x1, blocking collectives, on_device(): all_docs = lax.all_gather(segments, ('head', 'blk'), axis=1, tiled=True)  66.7 us
    all_gather x1, waiting for transfers between devices, on_device(): lax.all_gather(up_weight, ('head', 'blk'), axis=0, tiled=True)  62.9 us
  transfers between devices with their start and end apart: 19, of which 13 were waited for; matrix products, arithmetic and copies ran while one was open for 14% of the time, Pallas kernels for 0%

profile of v1, /device:TPU:0, one launch (start us, length us, event | category | flops | bytes accessed | tf_op | source)
XLA Modules:
  0.0 1186.8 jit_solution(13346700153040810410)
XLA Ops:
  7.2 6.4 collective-permute-start
  17.8 6.2 collective-permute-done.1
  26.7 20.8 %collective-permute-done.2 = bf16[96,2304]{1,0:T(8,128)(2,1)S(1)} collective-permute-done((bf16[96,2304]{1,0:T(8,128)(2,1)S(1)}, bf16[96,2304]{1,0:T(8,128)(2,1)S(1)}, u32[]{:S(2)}, u32[]{:S(2)}) %collective-permute-start.2) | collective-permute-done | bytes 442400 | tf_op jit(solution)/shard_map/ppermute | solution.py:24
  51.8 9.1 collective-permute-done.3
  65.0 77.1 %all-reduce.11 = (bf16[4608]{0:T(1024)(128)(2,1)S(1)}, bf16[768]{0:T(1024)(128)(2,1)S(1)}, bf16[768]{0:T(1024)(128)(2,1)S(1)}, bf16[3072]{0:T(1024)(128)(2,1)S(1)}, bf16[768]{0:T(1024)(128)(2,1)S(1)}) all-reduce(bf16[4608]{0:T(1024)(128)(2,1)S(1)} %dynamic-update-slice, ...), channel_id=1, replica_groups=mesh['head'=4,'blk'=8] {'head','blk'}, use_global_device_ids=true, to_apply=%add | all-reduce | flops 9984 | bytes 39936
  158.5 12.9 %all_to_all.69 = bf16[4,2,36864]{2,1,0:T(2,128)(2,1)S(1)} all-to-all(bf16[4,2,36864]{2,1,0:T(2,128)(2,1)S(1)} %reshape.208), channel_id=1, replica_groups=mesh['head'=4,'blk'=8] {'head'}, dimensions={0} | all-to-all | bytes 1179648 | tf_op jit(solution)/shard_map/all_to_all | solution.py:135
  178.6 38.9 %psum.15 = f32[]{:T(128)} all-reduce(f32[]{:T(128)} %convert_reduce_fusion.4), channel_id=1, replica_groups=mesh['head'=4,'blk'=8] {'head','blk'}, use_global_device_ids=true, to_apply=%region_9.10 | all-reduce | flops 1 | bytes 8 | tf_op jit(solution)/shard_map/psum | solution.py:199
  218.1 66.7 %all-gather.3 = s32[32,64,2]{1,2,0:T(2,128)S(1)} all-gather(s32[1,64,2]{1,2,0:T(2,128)S(1)} %bitcast.271), channel_id=1, replica_groups=mesh['head'=4,'blk'=8] {'head','blk'}, dimensions={0}, use_global_device_ids=true | all-gather | bytes 16896 | tf_op jit(solution)/shard_map/all_gather | solution.py:84
  294.1 5.9 select_reduce_fusion
  300.0 7.0 fusion
  307.0 6.9 fusion.77
  319.3 5.1 all-to-all-done.1
  324.9 6.1 all-gather.15.cloned.1.call-done
  333.6 62.9 %all-gather.17.cloned.1.call-done = bf16[768,3072]{1,0:T(8,128)(2,1)} async-done(((bf16[24,3072]{1,0:T(8,128)(2,1)}), bf16[768,3072]{1,0:T(8,128)(2,1)}) %all-gather.17.cloned.1.call-update) | async-done | bytes 4718608 | tf_op jit(solution)/shard_map/all_gather | solution.py:96
  399.7 62.0 %all-gather.19.cloned.1.call-done = bf16[3072,768]{1,0:T(8,128)(2,1)} async-done(((bf16[96,768]{1,0:T(8,128)(2,1)}), bf16[3072,768]{1,0:T(8,128)(2,1)}) %all-gather.19.cloned.1.call-update) | async-done | bytes 4718608 | tf_op jit(solution)/shard_map/all_gather | solution.py:97
  461.8 4.9 convert_reduce_fusion.2
  477.4 9.4 all_to_all.70
  496.5 15.6 %all-gather.27.cloned.1.call-done = bf16[2,2048,1,192]{3,1,2,0:T(8,128)(2,1)} async-done(((bf16[2,256,1,192]{3,1,2,0:T(8,128)(2,1)}), bf16[2,2048,1,192]{3,1,2,0:T(8,128)(2,1)}) %all-gather.27.cloned.1.call-update) | async-done | bytes 1572880 | tf_op jit(solution)/shard_map/all_gather | solution.py:296
  516.6 7.8 fusion.105
  531.5 20.2 %all_gather.60 = bf16[2,2048,18]{1,0,2:T(2,128)(2,1)S(1)} all-gather(bf16[2,256,18]{1,0,2:T(2,128)(2,1)S(1)} %bitcast.262), channel_id=1, replica_groups=mesh['head'=4,'blk'=8] {'blk'}, dimensions={1}, use_global_device_ids=true | all-gather | bytes 165888 | tf_op jit(solution)/shard_map/all_gather | solution.py:298
  553.1 12.1 %fusion.54 = bf16[2,3,256,64]{2,3,1,0:T(8,128)(2,1)} fusion(bf16[2,3,2048,64]{2,3,1,0:T(8,128)(2,1)} %bitcast.231, f32[2,3,256,2048]{3,2,1,0:T(8,128)} %get-tuple-element.73, f32[2,3,256]{2,1,0:T(4,128)S(1)} %multiply_reduce_fusion.4, f32[2,3,256]{2,1,0:T(4,128)} %log_add_fusion, pred[2,256,2048]{2,1,0:T(8,128)(4,1)S(1)} %broadcast_compare_fusion.1, ...), kind=kOutput, calls=%fused_computation.60 | convolution fusion | flops 824377344 | bytes 17182720 | tf_op jit(solution)/shard_map/shqk,shke->shqe/dot_general | solution.py:243
  571.1 7.4 fusion.56
  580.2 11.7 fusion.55
  596.1 14.5 %all_to_all.71 = bf16[2,256,3,192]{3,0,2,1:T(2,128)(2,1)S(1)} all-to-all(bf16[2,256,3,192]{3,0,2,1:T(2,128)(2,1)S(1)} %pad_maximum_fusion.1), channel_id=1, replica_groups=mesh['head'=4,'blk'=8] {'head'}, dimensions={1} | all-to-all | bytes 1179648 | tf_op jit(solution)/shard_map/all_to_all | solution.py:309
  619.5 5.3 convolution_bitcast_fusion
  624.9 5.1 convolution_bitcast_fusion.2
  631.0 5.2 convolution_bitcast_fusion.1
  642.2 37.8 %all-reduce.10 = (f32[]{:T(128)}, f32[4608]{0:T(1024)S(1)}, f32[768]{0:T(1024)S(1)}, f32[768]{0:T(1024)S(1)}, f32[3072]{0:T(1024)S(1)}, /*index=5*/f32[768]{0:T(1024)S(1)}) all-reduce(f32[]{:T(128)} %get-tuple-element.51, f32[4608]{0:T(1024)S(1)} %reduce_sum.238, ...), channel_id=1, replica_groups=mesh['head'=4,'blk'=8] {'head','blk'}, use_global_device_ids=true, to_apply=%region_7.8 | all-reduce | flops 9985 | bytes 79880 | tf_op jit(solution)/shard_map/psum | solution.py:199
  684.6 86.9 %reduce-scatter.6.cloned.1.call-done = f32[128,144]{0,1:T(8,128)} async-done(((f32[128,4608]{0,1:T(8,128)}), f32[128,144]{0,1:T(8,128)}) %reduce-scatter.6.cloned.1.call-update) | async-done | bytes 73744 | tf_op jit(solution)/shard_map/reduce_scatter | solution.py:342
  771.4 141.2 %reduce-scatter.12.cloned.1.call-done = f32[24,3072]{1,0:T(8,128)} async-done(((f32[768,3072]{1,0:T(8,128)}), f32[24,3072]{1,0:T(8,128)}) %reduce-scatter.12.cloned.1.call-update) | async-done | bytes 294928 | tf_op jit(solution)/shard_map/reduce_scatter | solution.py:333
  912.7 141.8 %reduce-scatter.14.cloned.1.call-done = f32[96,768]{1,0:T(8,128)} async-done(((f32[3072,768]{1,0:T(8,128)}), f32[96,768]{1,0:T(8,128)}) %reduce-scatter.14.cloned.1.call-update) | async-done | bytes 294928 | tf_op jit(solution)/shard_map/reduce_scatter | solution.py:334
  1054.4 124.5 %reduce-scatter.8.cloned.1.call-done = f32[24,2304]{1,0:T(8,128)} async-done(((f32[768,2304]{1,0:T(8,128)}), f32[24,2304]{1,0:T(8,128)}) %reduce-scatter.8.cloned.1.call-update) | async-done | bytes 221200 | tf_op jit(solution)/shard_map/reduce_scatter | solution.py:341
  (240 shorter events, 123.4 us)
Async XLA Ops:
  7.2 135.4 %copy-start = (f32[2,128]{1,0:T(2,128)S(1)}, f32[2,128]{1,0:T(2,128)}, u32[]{:S(2)}) copy-start(f32[2,128]{1,0:T(2,128)} %param.16) | copy-start | bytes 3076
  7.2 135.3 %all-gather.13.cloned.1.call-start = ((), (), s32[]{:S(2)}) async-start(), calls=%async_computation.9 | async-start | bytes 1216512 | tf_op jit(solution)/shard_map/all_gather | solution.py:98
  7.2 9.3 collective-permute-start
  17.4 6.6 collective-permute-start.1
  24.9 22.6 %collective-permute-start.2 = (bf16[96,2304]{1,0:T(8,128)(2,1)S(1)}, bf16[96,2304]{1,0:T(8,128)(2,1)S(1)}, u32[]{:S(2)}, u32[]{:S(2)}) collective-permute-start(bf16[96,2304]{1,0:T(8,128)(2,1)S(1)} %pad_maximum_fusion.2), channel_id=1, source_target_pairs={{0,28},{1,29},{2,30},{3,31},{4,0},{5,1},{6,2},{7,3},{8,4},{9,5},{1... | collective-permute-start | bytes 1327112 | tf_op jit(solution)/shard_map/ppermute | solution.py:24
  25.0 261.7 %all-gather.23.cloned.1.call-start = ((), (), s32[]{:S(2)}) async-start(), calls=%async_computation.19 | async-start | bytes 2359296 | tf_op jit(solution)/shard_map/all_gather | solution.py:173
  26.6 37.4 %copy-start.30 = (bf16[24]{0:T(256)(128)(2,1)S(1)}, bf16[24]{0:T(256)(128)(2,1)}, u32[]{:S(2)}) copy-start(bf16[24]{0:T(256)(128)(2,1)} %param.29) | copy-start | bytes 148
  26.6 37.6 %copy-start.31 = (bf16[24]{0:T(256)(128)(2,1)S(1)}, bf16[24]{0:T(256)(128)(2,1)}, u32[]{:S(2)}) copy-start(bf16[24]{0:T(256)(128)(2,1)} %param.25) | copy-start | bytes 148
  26.6 37.9 %copy-start.32 = (bf16[144]{0:T(256)(128)(2,1)S(1)}, bf16[144]{0:T(256)(128)(2,1)}, u32[]{:S(2)}) copy-start(bf16[144]{0:T(256)(128)(2,1)} %param.21) | copy-start | bytes 868
  26.7 38.1 %copy-start.33 = (bf16[96]{0:T(256)(128)(2,1)S(1)}, bf16[96]{0:T(256)(128)(2,1)}, u32[]{:S(2)}) copy-start(bf16[96]{0:T(256)(128)(2,1)} %param.27) | copy-start | bytes 580
  26.7 115.5 %copy-start.2 = (bf16[2,64,768]{2,1,0:T(8,128)(2,1)S(1)}, bf16[2,64,768]{2,1,0:T(8,128)(2,1)}, u32[]{:S(2)}) copy-start(bf16[2,64,768]{2,1,0:T(8,128)(2,1)} %param.15) | copy-start | bytes 589828
  48.5 12.5 %collective-permute-start.3 = (bf16[192,2304]{1,0:T(8,128)(2,1)S(1)}, bf16[192,2304]{1,0:T(8,128)(2,1)S(1)}, u32[]{:S(2)}, u32[]{:S(2)}) collective-permute-start(bf16[192,2304]{1,0:T(8,128)(2,1)S(1)} %pad_maximum_fusion), channel_id=1, source_target_pairs={{0,24},{1,25},{2,26},{3,27},{4,28},{5,29},{6,30},{7,31},{8,0},{9,1... | collective-permute-start | bytes 2654216 | tf_op jit(solution)/shard_map/ppermute | solution.py:24
  62.4 83.9 %copy-start.8 = (bf16[24,2304]{1,0:T(8,128)(2,1)S(1)}, bf16[24,2304]{1,0:T(8,128)(2,1)}, u32[]{:S(2)}) copy-start(bf16[24,2304]{1,0:T(8,128)(2,1)} %param.23) | copy-start | bytes 331780
  62.4 82.5 %collective-permute-start.4 = (bf16[384,2304]{1,0:T(8,128)(2,1)}, bf16[384,2304]{1,0:T(8,128)(2,1)S(1)}, u32[]{:S(2)}, u32[]{:S(2)}) collective-permute-start(bf16[384,2304]{1,0:T(8,128)(2,1)} %get-tuple-element.43), channel_id=1, source_target_pairs={{0,16},{1,17},{2,18},{3,19},{4,20},{5,21},{6,22},{7,23},{8,24},{9,... | collective-permute-start | bytes 5308424 | tf_op jit(solution)/shard_map/ppermute | solution.py:24
  172.2 45.9 %copy-start.26 = (s32[2,64]{1,0:T(2,128)S(1)}, s32[2,64]{1,0:T(2,128)}, u32[]{:S(2)}) copy-start(s32[2,64]{1,0:T(2,128)} %param.17) | copy-start | bytes 1540
  175.5 114.0 %copy-start.11 = (bf16[2,256,1,192]{3,1,2,0:T(8,128)(2,1)}, bf16[2,256,1,192]{3,1,2,0:T(8,128)(2,1)S(1)}, u32[]{:S(2)}) copy-start(bf16[2,256,1,192]{3,1,2,0:T(8,128)(2,1)S(1)} %get-tuple-element.48) | copy-start | bytes 589828
  175.5 114.0 %all-gather.25.cloned.1.call-start = ((), (), s32[]{:S(2)}) async-start(), calls=%async_computation.20 | async-start | bytes 2359296 | tf_op jit(solution)/shard_map/all_gather | solution.py:174
  176.3 154.7 %all-gather.15.cloned.1.call-start = ((), (), s32[]{:S(2)}) async-start(), calls=%async_computation.10 | async-start | bytes 1216512 | tf_op jit(solution)/shard_map/all_gather | solution.py:95
  176.9 219.6 %all-gather.17.cloned.1.call-start = ((), (), s32[]{:S(2)}) async-start(), calls=%async_computation.11 | async-start | bytes 4866048 | tf_op jit(solution)/shard_map/all_gather | solution.py:96
  177.4 284.3 %all-gather.19.cloned.1.call-start = ((), (), s32[]{:S(2)}) async-start(), calls=%async_computation.12 | async-start | bytes 4866048 | tf_op jit(solution)/shard_map/all_gather | solution.py:97
  285.8 175.9 %copy-start.22 = (f32[2,64]{1,0:T(2,128)}, f32[2,64]{1,0:T(2,128)S(1)}, u32[]{:S(2)}) copy-start(f32[2,64]{1,0:T(2,128)S(1)} %broadcast_multiply_fusion) | copy-start | bytes 1540
  314.8 9.6 all-to-all-start.1
  318.3 193.8 %all-gather.27.cloned.1.call-start = ((), (), s32[]{:S(2)}) async-start(), calls=%async_computation.21 | async-start | bytes 2359296 | tf_op jit(solution)/shard_map/all_gather | solution.py:296
  319.0 248.1 %all-gather.21.cloned.1.call-start = ((), (), s32[]{:S(2)}) async-start(), calls=%async_computation.13 | async-start | bytes 2359296 | tf_op jit(solution)/shard_map/all_gather | solution.py:297
  324.9 71.6 %copy-start.12 = (bf16[2,64,768]{2,1,0:T(8,128)(2,1)}, bf16[2,64,768]{2,1,0:T(8,128)(2,1)S(1)}, u32[]{:S(2)}) copy-start(bf16[2,64,768]{2,1,0:T(8,128)(2,1)S(1)} %all_to_all.57) | copy-start | bytes 589828
  396.5 65.3 %copy-start.28 = (bf16[2,64,768]{2,1,0:T(8,128)(2,1)S(1)}, bf16[2,64,768]{2,1,0:T(8,128)(2,1)}, u32[]{:S(2)}) copy-start(bf16[2,64,768]{2,1,0:T(8,128)(2,1)} %param.19) | copy-start | bytes 589828
  490.8 193.8 %reduce-scatter.10.cloned.1.call-start = ((), (), s32[]{:S(2)}) async-start(), calls=%async_computation.16 | async-start | bytes 2433024 | tf_op jit(solution)/shard_map/reduce_scatter | solution.py:332
  526.2 245.2 %reduce-scatter.6.cloned.1.call-start = ((), (), s32[]{:S(2)}) async-start(), calls=%async_computation.14 | async-start | bytes 2433024 | tf_op jit(solution)/shard_map/reduce_scatter | solution.py:342
  624.8 287.8 %reduce-scatter.12.cloned.1.call-start = ((), (), s32[]{:S(2)}) async-start(), calls=%async_computation.17 | async-start | bytes 9732096 | tf_op jit(solution)/shard_map/reduce_scatter | solution.py:333
  630.1 424.4 %reduce-scatter.14.cloned.1.call-start = ((), (), s32[]{:S(2)}) async-start(), calls=%async_computation.18 | async-start | bytes 9732096 | tf_op jit(solution)/shard_map/reduce_scatter | solution.py:334
  636.2 542.7 %reduce-scatter.8.cloned.1.call-start = ((), (), s32[]{:S(2)}) async-start(), calls=%async_computation.15 | async-start | bytes 7299072 | tf_op jit(solution)/shard_map/reduce_scatter | solution.py:341
  641.4 42.2 %copy-start.17 = (f32[2,64,768]{2,1,0:T(8,128)S(1)}, f32[2,64,768]{2,1,0:T(8,128)}, u32[]{:S(2)}) copy-start(f32[2,64,768]{2,1,0:T(8,128)} %get-tuple-element.79) | copy-start | bytes 1179652
  (23 other events, 132.7 us)
Sparse Core Ops, SparseCore 0:
  25.1 62.6 all-gather.12
  175.7 48.1 all-gather.22
  226.6 48.9 all-gather.24
  278.4 52.5 all-gather.14
  333.8 62.6 all-gather.16
  399.2 62.4 all-gather.18
  463.9 48.0 all-gather.26
  514.2 48.1 all-gather.20
  568.3 98.4 reduce-scatter.9
  673.3 98.0 reduce-scatter.5
  777.9 134.7 reduce-scatter.11
  920.0 134.3 reduce-scatter.13
  1060.7 118.1 reduce-scatter.7
